TPU v7x, 256 devices: a whole 4x4x8 slice. The times are simulated.
256 devices in a mesh: samp: 8 (over x, z_hi), feat: 32 (over y, z_lo, core).
Axes of the slice: x: 4, y: 4, z: 8 (z_hi: 2, z_lo: 4; z = z_hi * 4 + z_lo), core: 2. Of those that a mesh axis runs over, the one named last changes fastest.
Arguments:
- embeddings: bfloat16 [8192, 1024], P('samp'), may hold values from -6 to 6
- frequencies: bfloat16 [1024, 8192], P(None, 'feat'), may hold values from -0.1875 to 0.1875
- phases: float32 [8192], P('feat'), may hold values from -3.140625 to 3.140625
- treat_freq: float32 [8192], P('feat'), may hold values from -3.140625 to 3.140625
- treatment: int32 [8192], P('samp'), may hold values from 0 to 1
- flips: int32 [8192], P('samp'), may hold values from 0 to 1
- panel: int32 [1], replicated, may hold values from 0 to 15
Outputs:
- schur: float32 [8192, 8192], P('samp', 'feat')
- panel_factor: float32 [8192, 512], P('samp')
- moment_scaled: float32 [8192], P('feat')
All inputs are finite; a program needn't handle non-finite values.
Results may differ from a plain program's by a relative error of at most 0.0032.
Values may be sent and summed in bfloat16 or wider, within the bound.
No kernel may reach another device: no remote copies, remote signals or barrier semaphores. Data moves between devices by JAX's collectives and lax.ppermute only.
A program may use at most 128 MiB of HBM per device.

v0:
```python
import jax
import jax.numpy as jnp
from jax import lax
from jax.sharding import PartitionSpec as P

PANEL = 512
ridge = 0.1
root_two = 1.4142135623730951


def broadcast(shard, axis, root):
    mine = lax.axis_index(axis) == root
    return lax.psum(jnp.where(mine, shard, jnp.zeros_like(shard)), axis)


def cosine_map(project, phases, treat_freq, treated):
    return root_two * jnp.cos(project + phases[None, :] + treated[:, None] * treat_freq[None, :])


def inner_rows(left, right):
    return lax.dot_general(
        left, right, (((0,), (0,)), ((), ())), preferred_element_type=jnp.float32
    )


def per_device(embeddings, frequencies, phases, treat_freq, treatment, flips, panel):
    project = jnp.dot(embeddings, frequencies, preferred_element_type=jnp.float32)
    treated = treatment.astype(jnp.float32)
    flipped = flips.astype(jnp.float32)
    counter = treated + flipped - 2.0 * treated * flipped
    observed = cosine_map(project, phases, treat_freq, treated)
    counterfactual = cosine_map(project, phases, treat_freq, counter)
    feature_obs = observed.astype(jnp.bfloat16)
    samp_size = lax.axis_size("samp")
    feat_size = lax.axis_size("feat")
    sample_count = embeddings.shape[0] * samp_size
    col_width = feature_obs.shape[1]
    feat_total = col_width * feat_size
    row_height = feat_total // samp_size
    samp_index = lax.axis_index("samp")
    feat_index = lax.axis_index("feat")
    moment_part = jnp.sum(counterfactual - observed, axis=0)
    moment_sum = lax.psum(moment_part, "samp") / sample_count
    first_col = panel[0] * PANEL
    panel_devs = PANEL // col_width
    first_dev = first_col // col_width
    gram_part = inner_rows(lax.all_gather(feature_obs, "feat", axis=1, tiled=True), feature_obs)
    gram_raw = lax.psum_scatter(gram_part, "samp", scatter_dimension=0, tiled=True)
    row_ids = samp_index * row_height + lax.broadcasted_iota(jnp.int32, (row_height, col_width), 0)
    col_ids = feat_index * col_width + lax.broadcasted_iota(jnp.int32, (row_height, col_width), 1)
    gram_own = gram_raw / sample_count + ridge * (row_ids == col_ids).astype(jnp.float32)
    col_parts = []
    moment_parts = []
    for member in range(panel_devs):
        got_cols, got_moment = (
            broadcast(gram_own, "feat", first_dev + member),
            broadcast(moment_sum, "feat", first_dev + member),
        )
        col_parts.append(got_cols)
        moment_parts.append(got_moment)
    panel_cols = jnp.concatenate(col_parts, axis=1)
    moment_panel = jnp.concatenate(moment_parts, axis=0)
    source_samp = first_col // row_height
    offset_row = first_col % row_height
    pivot_local = lax.dynamic_slice_in_dim(panel_cols, offset_row, PANEL, 0)
    cross_local = lax.dynamic_slice_in_dim(gram_own, offset_row, PANEL, 0)
    pivot, cross = (
        broadcast(pivot_local, "samp", source_samp),
        broadcast(cross_local, "samp", source_samp),
    )
    lower = jnp.linalg.cholesky(pivot)
    factor_t = lax.linalg.triangular_solve(lower, panel_cols.T, left_side=True, lower=True)
    panel_factor = factor_t.T
    cross_t = lax.linalg.triangular_solve(lower, cross, left_side=True, lower=True)
    schur = gram_own - jnp.dot(panel_factor, cross_t, precision=lax.Precision.HIGHEST)
    solved = lax.linalg.triangular_solve(lower, moment_panel[:, None], left_side=True, lower=True)[
        :, 0
    ]
    reduced = moment_sum - jnp.dot(cross_t.T, solved, precision=lax.Precision.HIGHEST)
    moment_scaled = jnp.sqrt(jnp.float32(sample_count)) * reduced
    return (schur, panel_factor, moment_scaled)


def solution(mesh):
    return jax.shard_map(
        per_device,
        mesh=mesh,
        in_specs=(
            P("samp", None),
            P(None, "feat"),
            P("feat"),
            P("feat"),
            P("samp"),
            P("samp"),
            P(),
        ),
        out_specs=(P("samp", "feat"), P("samp", None), P("feat")),
        check_vma=False,
    )
```

profile of v0, /device:TPU:8, one launch (start us, length us, event | category | flops | bytes accessed | tf_op | source)
XLA Modules:
  0.0 977.7 jit_solution(12588586258870872119)
XLA Ops:
  8.8 9.7 subtract_reduce_fusion
  18.5 127.0 %all-gather.2.cloned.1.call-done = bf16[1024,8192]{1,0:T(8,128)(2,1)} async-done(((bf16[1024,256]{1,0:T(8,128)(2,1)}), bf16[1024,8192]{1,0:T(8,128)(2,1)}) %all-gather.2.cloned.1.call-update) | async-done | bytes 16777232 | tf_op jit(solution)/shard_map/all_gather | solution.py:47
  145.5 13.7 %fusion.87 = f32[8192,256]{0,1:T(8,128)} fusion(bf16[1024,8192]{1,0:T(8,128)(2,1)} %all-gather.2.cloned.1.call-done, bf16[1024,256]{1,0:T(8,128)(2,1)} %get-tuple-element.37), kind=kOutput, calls=%fused_computation.148 | convolution fusion | flops 4294967296 | bytes 25690112 | tf_op jit(solution)/shard_map/dot_general | solution.py:21
  160.0 184.1 %reduce-scatter.2.cloned.1.call-done = f32[1024,256]{0,1:T(8,128)} async-done(((f32[8192,256]{0,1:T(8,128)}), f32[1024,256]{0,1:T(8,128)}) %reduce-scatter.2.cloned.1.call-update) | async-done | bytes 1048592 | tf_op jit(solution)/shard_map/reduce_scatter | solution.py:48
  344.1 2.4 broadcast_select_fusion
  346.6 1.1 broadcast_select_fusion.1
  347.9 1.0 dynamic-slice_select_fusion.1
  348.9 263.1 %all-reduce.7.cloned.1.call-done = (f32[1024,256]{0,1:T(8,128)}, f32[1024,256]{0,1:T(8,128)}) async-done(((f32[1024,256]{0,1:T(8,128)}, f32[1024,256]{0,1:T(8,128)}), (f32[1024,256]{0,1:T(8,128)}, f32[1024,256]{0,1:T(8,128)})) %all-reduce.7.cloned.1.call-update) | async-done | bytes 2097168 | tf_op jit(solution)/shard_map/psum | solution.py:13
  612.0 1.4 constant_dynamic-update-slice_fusion.1
  613.6 1.3 copy-done.1
  614.9 1.3 dynamic-slice_select_fusion
  616.3 29.4 %psum.53 = f32[256]{0:T(256)S(1)} all-reduce(f32[256]{0:T(256)S(1)} %get-tuple-element.36), channel_id=1, replica_groups=mesh['samp'=8,'feat'=32] {'samp'}, use_global_device_ids=true, to_apply=%region_14.15 | all-reduce | flops 256 | bytes 2048 | tf_op jit(solution)/shard_map/psum | solution.py:43
  645.7 73.2 %all-reduce.1 = (f32[256]{0:T(256)S(1)}, f32[256]{0:T(256)S(1)}) all-reduce(f32[256]{0:T(256)S(1)} %get-tuple-element.45, f32[256]{0:T(256)S(1)} %get-tuple-element.44), channel_id=1, replica_groups=mesh['samp'=8,'feat'=32] {'feat'}, use_global_device_ids=true, to_apply=%region_15.16 | all-reduce | flops 512 | bytes 4096 | tf_op jit(solution)/shard_map/psum | solution.py:13
  719.4 72.7 %all-reduce.9.cloned.1.call-done = (f32[512,512]{0,1:T(8,128)}, f32[512,256]{0,1:T(8,128)}) async-done(((f32[512,512]{0,1:T(8,128)}, f32[512,256]{0,1:T(8,128)}), (f32[512,512]{0,1:T(8,128)}, f32[512,256]{0,1:T(8,128)})) %all-reduce.9.cloned.1.call-update) | async-done | bytes 1572880 | tf_op jit(solution)/shard_map/psum | solution.py:13
  792.2 2.6 copy.11
  794.8 1.4 fusion.19
  797.2 11.7 %cholesky.103 = f32[128,128]{1,0:T(8,128)S(1)} custom-call(f32[128,128]{1,0:T(8,128)S(1)} %cholesky.263), custom_call_target="Cholesky" | custom-call | tf_op jit(solution)/shard_map/jit(cholesky)/cholesky | solution.py:71
  809.0 9.8 %custom-call.34 = f32[1,128,128]{1,2,0:T(8,128)S(1)} custom-call(f32[1,128,128]{2,1,0:T(8,128)S(1)} %get-tuple-element.43), custom_call_target="InvertDiagBlocksLowerTriangular" | custom-call | tf_op jit(solution)/shard_map/jit(cholesky)/cholesky | solution.py:71
  818.8 1.2 fusion.35
  820.0 1.3 convolution_subtract_fusion.3
  821.3 11.7 %cholesky.215 = f32[128,128]{1,0:T(8,128)S(1)} custom-call(f32[128,128]{1,0:T(8,128)S(1)} %cholesky.267), custom_call_target="Cholesky" | custom-call | tf_op jit(solution)/shard_map/jit(cholesky)/cholesky | solution.py:71
  835.2 10.6 %custom-call.35 = f32[1,128,128]{1,2,0:T(8,128)} custom-call(f32[1,128,128]{2,1,0:T(8,128)S(1)} %get-tuple-element.41), custom_call_target="InvertDiagBlocksLowerTriangular" | custom-call | tf_op jit(solution)/shard_map/jit(cholesky)/cholesky | solution.py:71
  847.6 1.2 convolution_dynamic-update-slice_fusion
  848.7 1.5 convolution_subtract_fusion.6
  850.3 11.7 %cholesky.236 = f32[128,128]{1,0:T(8,128)S(1)} custom-call(f32[128,128]{1,0:T(8,128)S(1)} %cholesky.272), custom_call_target="Cholesky" | custom-call | tf_op jit(solution)/shard_map/jit(cholesky)/cholesky | solution.py:71
  862.1 9.8 %custom-call.36 = f32[1,128,128]{1,2,0:T(8,128)S(1)} custom-call(f32[1,128,128]{2,1,0:T(8,128)S(1)} %get-tuple-element.39), custom_call_target="InvertDiagBlocksLowerTriangular" | custom-call | tf_op jit(solution)/shard_map/jit(cholesky)/cholesky | solution.py:71
  872.2 1.3 convolution_subtract_fusion.8
  873.6 11.9 %cholesky.253 = f32[128,128]{1,0:T(8,128)S(1)} custom-call(f32[128,128]{1,0:T(8,128)S(1)} %convolution_subtract_fusion.8), custom_call_target="Cholesky" | custom-call | tf_op jit(solution)/shard_map/jit(cholesky)/cholesky | solution.py:71
  886.9 1.3 compare_reduce_fusion.2
  890.7 1.1 select_select_fusion
  891.8 14.1 %while.1 = (s32[]{:T(128)}, f32[512,512]{0,1:T(8,128)}, s32[4,2]{0,1:T(2,128)S(1)}, f32[4,128,128]{2,1,0:T(8,128)}, s32[]{:T(128)}) while((s32[]{:T(128)}, f32[512,512]{0,1:T(8,128)}, s32[4,2]{0,1:T(2,128)S(1)}, f32[4,128,128]{2,1,0:T(8,128)}, s32[]{:T(128)}) %tuple.32), condition=%wide.while_cond, body=%wide.while_body.sunk | while | flops 2 | bytes 393829 | solution.py:72
  892.4 2.2 dynamic-slice.7
  895.9 2.2 dynamic-slice.7
  899.5 2.2 dynamic-slice.7
  903.0 2.2 dynamic-slice.7
  905.9 40.2 %custom-call.37 = f32[4,128,128]{1,2,0:T(8,128)S(1)} custom-call(f32[4,128,128]{2,1,0:T(8,128)} %get-tuple-element.10), custom_call_target="InvertDiagBlocksLowerTriangular" | custom-call | tf_op jit(solution)/shard_map/triangular_solve | solution.py:72
  946.3 1.1 fusion.12
  947.6 1.1 fusion.13
  948.9 1.2 fusion.15
  950.2 1.2 fusion.40
  951.4 1.3 convolution_subtract_fusion.7
  953.1 1.6 convolution_subtract_fusion.5
  955.0 1.7 convolution_subtract_fusion.4
  960.4 1.1 fusion.6
  962.2 1.6 fusion.9
  963.8 2.0 convolution_subtract_fusion
  966.8 2.9 copy.22
  969.6 1.3 copy.21
  (87 shorter events, 21.2 us)
Async XLA Ops:
  7.2 1.6 copy-start
  7.2 138.3 %all-gather.2.cloned.1.call-start = ((), (), s32[]{:S(2)}) async-start(), calls=%async_computation.1 | async-start | bytes 17301504 | tf_op jit(solution)/shard_map/all_gather | solution.py:47
  18.5 325.7 %reduce-scatter.2.cloned.1.call-start = ((), (), s32[]{:S(2)}) async-start(), calls=%async_computation.2 | async-start | bytes 9437184 | tf_op jit(solution)/shard_map/reduce_scatter | solution.py:48
  159.2 452.7 %all-reduce.7.cloned.1.call-start = ((), (), s32[]{:S(2)}) async-start(), calls=%async_computation.3 | async-start | bytes 4194304 | tf_op jit(solution)/shard_map/psum | solution.py:13
  346.6 1.3 copy-start.3
  347.7 444.5 %all-reduce.9.cloned.1.call-start = ((), (), s32[]{:S(2)}) async-start(), calls=%async_computation.4 | async-start | bytes 3145728 | tf_op jit(solution)/shard_map/psum | solution.py:13
  612.0 1.5 copy-start.8
  613.6 1.3 copy-start.1
  792.2 2.6 copy-start.6
  796.3 1.0 copy-start.7
  848.7 43.0 %copy-start.9 = (s32[4]{0:T(128)S(1)}, s32[4]{0:T(128)}, u32[]{:S(2)}) copy-start(s32[4]{0:T(128)} %iota_multiply_fusion) | copy-start | bytes 52
  905.9 49.1 %copy-start.5 = (f32[512,512]{0,1:T(8,128)S(1)}, f32[512,512]{0,1:T(8,128)}, u32[]{:S(2)}) copy-start(f32[512,512]{0,1:T(8,128)} %get-tuple-element.104) | copy-start | bytes 3145732
  946.1 10.9 %copy-start.2 = (f32[1024,512]{0,1:T(8,128)S(1)}, f32[1024,512]{0,1:T(8,128)}, u32[]{:S(2)}) copy-start(f32[1024,512]{0,1:T(8,128)} %copy-done.1) | copy-start | bytes 6291460
  962.1 1.6 copy-start.4
Sparse Core Ops, SparseCore 0:
  18.6 126.8 all-gather.1
  159.4 184.7 reduce-scatter.1
  347.8 264.0 all-reduce.6
  616.4 175.7 all-reduce.8
where the time goes:
time: 985 us; the launch traced here: 978 us
  waiting for transfers between devices  647 us (66%)
  other arithmetic  133 us (14%)
  blocking collectives  103 us (10%)
  matrix products  48.4 us (5%)
  local copies, waits for them, and re-layouts  28.5 us (3%)
  between operations  17.5 us (2%)
    psum x2, waiting for transfers between devices, broadcast(): return lax.psum(jnp.where(mine, shard, jnp.zeros_like(shard)), axis)  336 us
    reduce_scatter x1, waiting for transfers between devices, per_device(): lax.psum_scatter(gram_part, 'samp', scatter_dimension=0, tiled=True)  184 us
    all_gather x1, waiting for transfers between devices, per_device(): lax.all_gather(feature_obs, 'feat', axis=1, tiled=True)  127 us
    another operation x14, other arithmetic, per_device(): lower = jnp.linalg.cholesky(pivot)  80.5 us
    psum x1, blocking collectives, broadcast(): return lax.psum(jnp.where(mine, shard, jnp.zeros_like(shard)), axis)  73.2 us
    another operation x3, other arithmetic, per_device(): lax.linalg.triangular_solve(lower, panel_cols.T, left_side=True, lower=True)  41.9 us
    psum x1, blocking collectives, per_device(): moment_sum = lax.psum(moment_part, 'samp') / sample_count  29.4 us
  transfers between devices with their start and end apart: 4, of which 4 were waited for; matrix products, arithmetic and copies ran while one was open for 0% of the time, Pallas kernels for 0%

commit v1 on v0

--- a/solution.py
+++ b/solution.py
@@ -2,6 +2,7 @@
 import jax.numpy as jnp
 from jax import lax
 from jax.sharding import PartitionSpec as P
+from jax.lax import all_gather
 
 PANEL = 512
 ridge = 0.1
@@ -10,7 +11,11 @@
 
 def broadcast(shard, axis, root):
     mine = lax.axis_index(axis) == root
-    return lax.psum(jnp.where(mine, shard, jnp.zeros_like(shard)), axis)
+
+    def _arrange_ranges(base_x):
+        return all_gather(base_x, axis_name=axis).sum(axis=0)
+
+    return _arrange_ranges(jnp.where(mine, shard, jnp.zeros_like(shard)))
 
 
 def cosine_map(project, phases, treat_freq, treated):

time: 985 us -> 1190 us (1.21)
  waiting for transfers between devices: 647 us -> 816 us
  other arithmetic: 133 us -> 173 us
  local copies, waits for them, and re-layouts: 28.5 us -> 14.8 us
    all_gather x0 -> x4, waiting for transfers between devices: none -> 504 us  [_arrange_ranges(): return all_gather(base_x, axis_name=axis).sum(axis=0)]
    psum x2 -> x0, waiting for transfers between devices: 336 us -> none  [broadcast(): return lax.psum(jnp.where(mine, shard, jnp.zeros_like(shard)), axis)]
    all_gather x0 -> x2, blocking collectives: none -> 77.4 us  [_arrange_ranges(): return all_gather(base_x, axis_name=axis).sum(axis=0)]
    psum x1 -> x0, blocking collectives: 73.2 us -> none  [broadcast(): return lax.psum(jnp.where(mine, shard, jnp.zeros_like(shard)), axis)]
    reduce_sum x0 -> x6, other arithmetic: none -> 31.8 us  [_arrange_ranges(): return all_gather(base_x, axis_name=axis).sum(axis=0)]
  transfers between devices with their start and end apart: 4 -> 6, of which waited for: 4 -> 5; matrix products, arithmetic and copies ran while one was open for 0% -> 3% of each run, Pallas kernels for 0% -> 0%
where the time goes in v1:
time: 1190 us; the launch traced here: 1180 us
  waiting for transfers between devices  816 us (69%)
  other arithmetic  173 us (15%)
  blocking collectives  113 us (9%)
  matrix products  48.4 us (4%)
  between operations  18.1 us (2%)
  local copies, waits for them, and re-layouts  14.8 us (1%)
    all_gather x4, waiting for transfers between devices, _arrange_ranges(): return all_gather(base_x, axis_name=axis).sum(axis=0)  504 us
    reduce_scatter x1, waiting for transfers between devices, per_device(): lax.psum_scatter(gram_part, 'samp', scatter_dimension=0, tiled=True)  184 us
    all_gather x1, waiting for transfers between devices, per_device(): lax.all_gather(feature_obs, 'feat', axis=1, tiled=True)  127 us
    another operation x14, other arithmetic, per_device(): lower = jnp.linalg.cholesky(pivot)  89.9 us
    all_gather x2, blocking collectives, _arrange_ranges(): return all_gather(base_x, axis_name=axis).sum(axis=0)  77.4 us
    another operation x3, other arithmetic, per_device(): lax.linalg.triangular_solve(lower, panel_cols.T, left_side=True, lower=True)  40.5 us
    psum x1, blocking collectives, per_device(): moment_sum = lax.psum(moment_part, 'samp') / sample_count  35.5 us
    reduce_sum x6, other arithmetic, _arrange_ranges(): return all_gather(base_x, axis_name=axis).sum(axis=0)  31.8 us
  transfers between devices with their start and end apart: 6, of which 5 were waited for; matrix products, arithmetic and copies ran while one was open for 3% of the time, Pallas kernels for 0%

profile of v1, /device:TPU:8, one launch (start us, length us, event | category | flops | bytes accessed | tf_op | source)
XLA Modules:
  0.0 1183.2 jit_solution(3955284008430421817)
XLA Ops:
  7.2 0.8 convert_element_type.10
  8.1 0.7 multiply_subtract_fusion
  8.8 9.7 subtract_reduce_fusion
  18.5 127.0 %all-gather.14.cloned.1.call-done = bf16[1024,8192]{1,0:T(8,128)(2,1)} async-done(((bf16[1024,256]{1,0:T(8,128)(2,1)}), bf16[1024,8192]{1,0:T(8,128)(2,1)}) %all-gather.14.cloned.1.call-update) | async-done | bytes 16777232 | tf_op jit(solution)/shard_map/all_gather | solution.py:52
  145.5 13.8 %fusion.90 = f32[8192,256]{1,0:T(8,128)} fusion(bf16[1024,8192]{1,0:T(8,128)(2,1)} %all-gather.14.cloned.1.call-done, bf16[1024,256]{1,0:T(8,128)(2,1)} %get-tuple-element.30), kind=kOutput, calls=%fused_computation.151 | convolution fusion | flops 4294967296 | bytes 25690112 | tf_op jit(solution)/shard_map/dot_general | solution.py:26
  160.1 184.1 %reduce-scatter.2.cloned.1.call-done = f32[1024,256]{1,0:T(8,128)} async-done(((f32[8192,256]{1,0:T(8,128)}), f32[1024,256]{1,0:T(8,128)}) %reduce-scatter.2.cloned.1.call-update) | async-done | bytes 1048592 | tf_op jit(solution)/shard_map/reduce_scatter | solution.py:53
  344.2 2.4 broadcast_select_fusion.1
  346.6 1.0 broadcast_select_fusion
  348.3 0.8 dynamic-slice_select_fusion
  349.2 177.1 %all-gather.18.cloned.1.call-done = f32[32768,256]{1,0:T(8,128)} async-done(((f32[1024,256]{1,0:T(8,128)}), f32[32768,256]{1,0:T(8,128)}) %all-gather.18.cloned.1.call-update) | async-done | bytes 33554448 | tf_op jit(solution)/shard_map/all_gather | solution.py:16
  526.3 11.9 %reduce_sum.64 = f32[1024,256]{1,0:T(8,128)S(1)} reduce(f32[32,1024,256]{2,1,0:T(8,128)} %bitcast.125, f32[]{:T(128)} %constant.208.clone.1), dimensions={0}, to_apply=%region_2.3 | reduce | flops 8126464 | bytes 34603012 | tf_op jit(solution)/shard_map/reduce_sum | solution.py:16
  538.3 175.3 %all-gather.16.cloned.1.call-done = f32[32768,256]{1,0:T(8,128)} async-done(((f32[1024,256]{1,0:T(8,128)}), f32[32768,256]{1,0:T(8,128)}) %all-gather.16.cloned.1.call-update) | async-done | bytes 33554448 | tf_op jit(solution)/shard_map/all_gather | solution.py:16
  713.6 11.9 %reduce_sum.63 = f32[1024,256]{1,0:T(8,128)S(1)} reduce(f32[32,1024,256]{2,1,0:T(8,128)} %bitcast.126, f32[]{:T(128)} %constant.208.clone.1), dimensions={0}, to_apply=%region_1.0 | reduce | flops 8126464 | bytes 34603012 | tf_op jit(solution)/shard_map/reduce_sum | solution.py:16
  725.5 1.1 fusion.18
  726.7 35.5 %psum.7 = f32[256]{0:T(256)S(1)} all-reduce(f32[256]{0:T(256)S(1)} %get-tuple-element.29), channel_id=1, replica_groups=mesh['samp'=8,'feat'=32] {'samp'}, use_global_device_ids=true, to_apply=%region_14.15 | all-reduce | flops 256 | bytes 2048 | tf_op jit(solution)/shard_map/psum | solution.py:48
  762.2 40.9 %all-gather.6 = f32[32,1,256]{2,1,0:T(1,128)S(1)} all-gather(f32[1,1,256]{2,1,0:T(1,128)S(1)} %bitcast.130), channel_id=6, replica_groups=mesh['samp'=8,'feat'=32] {'feat'}, dimensions={0}, use_global_device_ids=true | all-gather | bytes 33792 | tf_op jit(solution)/shard_map/all_gather | solution.py:16
  803.2 36.4 %all-gather.7 = f32[32,1,256]{2,1,0:T(1,128)S(1)} all-gather(f32[1,1,256]{2,1,0:T(1,128)S(1)} %bitcast.129), channel_id=7, replica_groups=mesh['samp'=8,'feat'=32] {'feat'}, dimensions={0}, use_global_device_ids=true | all-gather | bytes 33792 | tf_op jit(solution)/shard_map/all_gather | solution.py:16
  839.7 3.4 reduce_sum.66
  843.1 1.6 fusion
  844.7 151.4 %all-gather.20.cloned.1.call-done = f32[4096,512]{1,0:T(8,128)} async-done(((f32[512,512]{1,0:T(8,128)}), f32[4096,512]{1,0:T(8,128)}) %all-gather.20.cloned.1.call-update) | async-done | bytes 8388624 | tf_op jit(solution)/shard_map/all_gather | solution.py:16
  996.1 4.5 reduce_sum.65
  1001.2 1.0 copy-done.3
  1002.2 11.7 cholesky.103
  1014.1 9.8 custom-call.34
  1023.9 1.2 constant_dynamic-update-slice_fusion
  1025.1 1.3 convolution_subtract_fusion.3
  1026.4 23.2 %cholesky.215 = f32[128,128]{1,0:T(8,128)S(1)} custom-call(f32[128,128]{1,0:T(8,128)S(1)} %cholesky.267), custom_call_target="Cholesky" | custom-call | tf_op jit(solution)/shard_map/jit(cholesky)/cholesky | solution.py:76
  1049.6 9.8 custom-call.35
  1059.7 1.3 convolution_subtract_fusion.6
  1061.0 11.7 cholesky.236
  1073.5 9.8 custom-call.36
  1083.5 1.2 convolution_subtract_fusion.8
  1084.7 11.7 cholesky.253
  1100.5 10.4 while.1
  1101.1 2.0 bitcast_dynamic-update-slice_fusion.2
  1103.7 2.0 bitcast_dynamic-update-slice_fusion.2
  1106.3 2.0 bitcast_dynamic-update-slice_fusion.2
  1108.9 2.0 bitcast_dynamic-update-slice_fusion.2
  1110.9 40.3 %custom-call.37 = f32[4,128,128]{1,2,0:T(8,128)S(1)} custom-call(f32[4,128,128]{2,1,0:T(8,128)} %get-tuple-element.10), custom_call_target="InvertDiagBlocksLowerTriangular" | custom-call | tf_op jit(solution)/shard_map/triangular_solve | solution.py:77
  1152.7 1.2 fusion.43
  1153.9 1.3 convolution_subtract_fusion.7
  1156.9 1.7 fusion.24
  1158.6 1.0 convolution_subtract_fusion.2
  1160.2 1.8 convolution_subtract_fusion.1
  1162.7 2.7 fusion.7
  1166.1 1.6 fusion.10
  1167.7 4.5 convolution_subtract_fusion
  1173.1 2.9 copy.13
  (71 shorter events, 12.7 us)
Async XLA Ops:
  7.2 1.6 copy-start
  7.2 138.3 %all-gather.14.cloned.1.call-start = ((), (), s32[]{:S(2)}) async-start(), calls=%async_computation.1 | async-start | bytes 17301504 | tf_op jit(solution)/shard_map/all_gather | solution.py:52
  18.5 325.7 %reduce-scatter.2.cloned.1.call-start = ((), (), s32[]{:S(2)}) async-start(), calls=%async_computation.2 | async-start | bytes 9437184 | tf_op jit(solution)/shard_map/reduce_scatter | solution.py:53
  159.3 367.0 %all-gather.18.cloned.1.call-start = ((), (), s32[]{:S(2)}) async-start(), calls=%async_computation.4 | async-start | bytes 34603008 | tf_op jit(solution)/shard_map/all_gather | solution.py:16
  347.6 366.0 %all-gather.16.cloned.1.call-start = ((), (), s32[]{:S(2)}) async-start(), calls=%async_computation.3 | async-start | bytes 34603008 | tf_op jit(solution)/shard_map/all_gather | solution.py:16
  348.2 491.5 %all-gather.22.cloned.1.call-start = ((), (), s32[]{:S(2)}) async-start(), calls=%async_computation.6 | async-start | bytes 4718592 | tf_op jit(solution)/shard_map/all_gather | solution.py:16
  349.2 646.9 %all-gather.20.cloned.1.call-start = ((), (), s32[]{:S(2)}) async-start(), calls=%async_computation.5 | async-start | bytes 9437184 | tf_op jit(solution)/shard_map/all_gather | solution.py:16
  1001.2 1.0 copy-start.3
  1100.5 55.1 %copy-start.4 = (f32[512,256]{1,0:T(8,128)S(1)}, f32[512,256]{1,0:T(8,128)}, u32[]{:S(2)}) copy-start(f32[512,256]{1,0:T(8,128)} %reduce_sum.66) | copy-start | bytes 1572868
  1153.9 4.7 copy-start.2
  1172.4 3.6 copy-start.1
Sparse Core Ops, SparseCore 0:
  18.6 126.8 all-gather.13
  159.4 184.6 reduce-scatter.1
  347.8 178.5 all-gather.17
  528.6 184.9 all-gather.15
  716.1 108.9 all-gather.21
  828.1 167.9 all-gather.19
